TPU v7x, 128 devices: a whole 4x4x4 slice. The times are simulated.
128 devices in a mesh: sn: 32 (over x, y, core), rhs: 4 (over z).
Axes of the slice: x: 4, y: 4, z: 4, core: 2. Of those that a mesh axis runs over, the one named last changes fastest.
Arguments:
- rhs_leaf: float32 [1024, 256, 128], P('sn', 'rhs'), may hold values from -6 to 6
- rhs_top: float32 [32, 256, 128], P('sn', 'rhs'), may hold values from -6 to 6
- leaf_blocks: float32 [1024, 3, 128, 128], P('sn', None, 'rhs'), may hold values from -0.078125 to 0.078125
- leaf_dinv: float32 [1024, 128, 128], P('sn', 'rhs')
- leaf_struct: int32 [1024, 3], P('sn'), may hold values from 1 to 63, as said below
- top_blocks: float32 [32, 32, 128, 128], P(None, 'sn', 'rhs'), may hold values from -0.1875 to 0.1875
- top_dinv: float32 [32, 128, 128], P('sn', 'rhs')
Outputs:
- leaf_solution: float32 [1024, 256, 128], P('sn', 'rhs')
- top_solution: float32 [32, 256, 128], P('sn', 'rhs')
Inputs may be any that keep to these rules, and one draw needn't show every extreme that they name: `leaf_struct`: subtree d hangs below top supernode a = 4 * (d // 4). Row d * 32 + s names 3 distinct ancestors of leaf supernode s of subtree d: a value v < 32 is supernode v of the same subtree, with v > s; a value 32 + k is a top supernode k on a's path to the root, that is k = a or the factor holds top block (k, a). Column 0 is the elimination tree parent: s + 1, except for the subtree's last supernode, whose parent is 32 + a.
All inputs are finite; a program needn't handle non-finite values.
Results may differ from a plain program's by a relative error of at most 0.00018.
Values sent between devices are 32-bit elements; how exact they have to be, the bound alone decides.
A program may use at most 64 MiB of HBM per device.

v0:
```python
import jax
import jax.numpy as jnp
from jax import lax
from jax.sharding import PartitionSpec as P

highest = lax.Precision.HIGHEST


def top_levels(count):
    levels = count.bit_length()
    index = jnp.arange(count, dtype=jnp.int32)
    depth_of = jnp.zeros((count,), jnp.int32)
    span = jnp.ones((count,), jnp.int32)
    for place in range(levels):
        hit = ((index + 1) % 2 ** (place + 1) == 0).astype(jnp.int32)
        depth_of = depth_of + hit
        span = span + hit * 2**place
    row_index = index[:, None]
    col_index = index[None, :]
    keep = (col_index < row_index) & (col_index >= row_index + 1 - span[:, None])
    return (depth_of, keep.astype(jnp.float32))


def leaf_forward(top_total, rhs_part, blocks, inverses, struct):
    leaf_total = rhs_part.shape[0]
    updates = jnp.zeros((leaf_total + top_total,) + rhs_part.shape[1:], jnp.float32)
    values = jnp.zeros(rhs_part.shape, jnp.float32)

    def advance(position, state_pair):
        updates, values = state_pair
        source = lax.dynamic_index_in_dim(rhs_part, position, 0, False) - lax.dynamic_index_in_dim(
            updates, position, 0, False
        )
        solved = jnp.einsum(
            "ck,ik->ci",
            source,
            lax.dynamic_index_in_dim(inverses, position, 0, False),
            precision=highest,
        )
        targets = lax.dynamic_index_in_dim(struct, position, 0, False)
        outgoing = jnp.einsum(
            "ck,rik->rci",
            solved,
            lax.dynamic_index_in_dim(blocks, position, 0, False),
            precision=highest,
        )
        updates = updates.at[targets].add(outgoing)
        values = lax.dynamic_update_index_in_dim(values, solved, position, 0)
        return (updates, values)

    updates, values = lax.fori_loop(0, leaf_total, advance, (updates, values))
    return (values, updates[leaf_total:])


def leaf_backward(forward_values, blocks, inverses, struct, top_values):
    leaf_total = forward_values.shape[0]
    solution_buffer = jnp.concatenate([jnp.zeros_like(forward_values), top_values], axis=0)

    def retreat(offset, solution_buffer):
        position = leaf_total - 1 - offset
        targets = lax.dynamic_index_in_dim(struct, position, 0, False)
        ancestors = jnp.take(solution_buffer, targets, axis=0)
        summed = jnp.einsum(
            "rci,rik->ck",
            ancestors,
            lax.dynamic_index_in_dim(blocks, position, 0, False),
            precision=highest,
        )
        own_rhs = lax.dynamic_index_in_dim(forward_values, position, 0, False)
        solved = jnp.einsum(
            "ci,ik->ck",
            own_rhs - summed,
            lax.dynamic_index_in_dim(inverses, position, 0, False),
            precision=highest,
        )
        return lax.dynamic_update_index_in_dim(solution_buffer, solved, position, 0)

    solution_buffer = lax.fori_loop(0, leaf_total, retreat, solution_buffer)
    return solution_buffer[:leaf_total]


def forward_by_rows(top_source, masked_rows, own_inverse, my_level, levels, pull_values):
    forward_own = jnp.zeros_like(top_source)
    for level in range(levels):
        if level == 0:
            pulled = jnp.zeros_like(top_source)
        else:
            gathered = pull_values(forward_own[None])
            pulled = jnp.einsum("jck,jik->ci", gathered, masked_rows, precision=highest)
        candidate = jnp.einsum("ck,ik->ci", top_source - pulled, own_inverse, precision=highest)
        forward_own = jnp.where(my_level == level, candidate, forward_own)
    return forward_own


def backward_by_rows(forward_own, masked_rows, own_inverse, my_level, levels, sum_terms):
    backward_own = jnp.zeros_like(forward_own)
    pushed = jnp.zeros_like(forward_own)
    for level in range(levels - 1, -1, -1):
        candidate = jnp.einsum("ci,ik->ck", forward_own - pushed, own_inverse, precision=highest)
        backward_own = jnp.where(my_level == level, candidate, backward_own)
        if level > 0:
            sender = (my_level == level).astype(jnp.float32)
            outgoing = (
                jnp.einsum("ci,tik->tck", backward_own, masked_rows, precision=highest) * sender
            )
            pushed = pushed + sum_terms(outgoing)[0]
    return backward_own


def local(rhs_leaf, rhs_top, leaf_blocks, leaf_dinv, leaf_struct, top_blocks, top_dinv):
    blocks, inverses, top_cols, top_inverse = (
        lax.all_gather(leaf_blocks, "rhs", axis=2, tiled=True),
        lax.all_gather(leaf_dinv, "rhs", axis=1, tiled=True),
        lax.all_gather(top_blocks, "rhs", axis=2, tiled=True),
        lax.all_gather(top_dinv, "rhs", axis=1, tiled=True),
    )
    top_total = top_cols.shape[0]
    levels = top_total.bit_length()
    my_index = lax.axis_index("sn")
    depth_of, keep = top_levels(top_total)
    my_level = lax.dynamic_index_in_dim(depth_of, my_index, 0, False)
    own_inverse = top_inverse[0]
    forward_leaf, leaf_updates = leaf_forward(top_total, rhs_leaf, blocks, inverses, leaf_struct)
    own_update = lax.psum_scatter(leaf_updates, "sn", scatter_dimension=0, tiled=True)
    top_source = rhs_top[0] - own_update[0]
    keep_row = lax.dynamic_index_in_dim(keep, my_index, 0, False)
    row_blocks = lax.all_to_all(top_cols, "sn", split_axis=0, concat_axis=1, tiled=True)
    masked_rows = row_blocks[0] * keep_row[:, None, None]
    forward_own = forward_by_rows(
        top_source,
        masked_rows,
        own_inverse,
        my_level,
        levels,
        lambda stacked: lax.all_gather(stacked, "sn", axis=0, tiled=True),
    )
    backward_own = backward_by_rows(
        forward_own,
        masked_rows,
        own_inverse,
        my_level,
        levels,
        lambda stacked: lax.psum_scatter(stacked, "sn", scatter_dimension=0, tiled=True),
    )
    all_top = lax.all_gather(backward_own[None], "sn", axis=0, tiled=True)
    leaf_solution = leaf_backward(forward_leaf, blocks, inverses, leaf_struct, all_top)
    return (leaf_solution, backward_own[None])


def solution(mesh):
    return jax.shard_map(
        local,
        mesh=mesh,
        in_specs=(
            P("sn", "rhs", None),
            P("sn", "rhs", None),
            P("sn", None, "rhs", None),
            P("sn", "rhs", None),
            P("sn", None),
            P(None, "sn", "rhs", None),
            P("sn", "rhs", None),
        ),
        out_specs=(P("sn", "rhs", None), P("sn", "rhs", None)),
        check_vma=False,
    )
```

profile of v0, /device:TPU:1, one launch (start us, length us, event | category | flops | bytes accessed | tf_op | source)
XLA Modules:
  0.0 1077.8 jit_solution(17331218211384969366)
XLA Ops:
  9.5 34.2 %all-gather.18.cloned.1.call-done = f32[32,128,128]{2,1,0:T(8,128)} async-done(((f32[32,32,128]{2,1,0:T(8,128)}), f32[32,128,128]{2,1,0:T(8,128)}) %all-gather.18.cloned.1.call-update) | async-done | bytes 2097168 | tf_op jit(solution)/shard_map/all_gather | solution.py:113
  43.7 67.4 %all-gather.16.cloned.1.call-done = f32[32,3,128,128]{3,2,1,0:T(8,128)} async-done(((f32[32,3,32,128]{3,2,1,0:T(8,128)}), f32[32,3,128,128]{3,2,1,0:T(8,128)}) %all-gather.16.cloned.1.call-update) | async-done | bytes 6291472 | tf_op jit(solution)/shard_map/all_gather | solution.py:112
  111.4 100.6 %while.30 = (s32[]{:T(128)}, f32[64,64,128]{2,1,0:T(8,128)S(1)}, f32[32,64,128]{2,1,0:T(8,128)S(1)}, s32[32,3]{1,0:T(8,128)S(1)}, f32[32,3,128,128]{3,2,1,0:T(8,...) while((s32[]{:T(128)}, f32[64,64,128]{2,1,0:T(8,128)S(1)}, ...), condition=%wide.region_2.3_spmd, body=%wide.region_0.2_spmd.sunk | while | flops 50364424 | bytes 821373 | solution.py:51
  112.5 1.3 convolution_bitcast_fusion.9
  115.6 1.3 convolution_bitcast_fusion.9
  118.8 1.3 convolution_bitcast_fusion.9
  121.9 1.3 convolution_bitcast_fusion.9
  125.1 1.3 convolution_bitcast_fusion.9
  128.2 1.3 convolution_bitcast_fusion.9
  131.4 1.3 convolution_bitcast_fusion.9
  134.5 1.3 convolution_bitcast_fusion.9
  137.7 1.3 convolution_bitcast_fusion.9
  140.8 1.3 convolution_bitcast_fusion.9
  144.0 1.3 convolution_bitcast_fusion.9
  147.1 1.3 convolution_bitcast_fusion.9
  150.3 1.3 convolution_bitcast_fusion.9
  153.4 1.3 convolution_bitcast_fusion.9
  156.6 1.3 convolution_bitcast_fusion.9
  159.7 1.3 convolution_bitcast_fusion.9
  162.8 1.3 convolution_bitcast_fusion.9
  166.0 1.3 convolution_bitcast_fusion.9
  169.1 1.3 convolution_bitcast_fusion.9
  172.3 1.3 convolution_bitcast_fusion.9
  175.4 1.3 convolution_bitcast_fusion.9
  178.6 1.3 convolution_bitcast_fusion.9
  181.7 1.3 convolution_bitcast_fusion.9
  184.8 1.3 convolution_bitcast_fusion.9
  188.0 1.3 convolution_bitcast_fusion.9
  191.1 1.3 convolution_bitcast_fusion.9
  194.3 1.3 convolution_bitcast_fusion.9
  197.4 1.3 convolution_bitcast_fusion.9
  200.6 1.3 convolution_bitcast_fusion.9
  203.7 1.3 convolution_bitcast_fusion.9
  206.9 1.3 convolution_bitcast_fusion.9
  210.0 1.3 convolution_bitcast_fusion.9
  214.5 9.0 all_gather.32
  223.5 10.7 all-to-all-start
  234.3 55.7 %reduce-scatter.7.cloned.1.call-done = f32[1,64,128]{2,1,0:T(8,128)} async-done(((f32[32,64,128]{2,1,0:T(8,128)}), f32[1,64,128]{2,1,0:T(8,128)}) %reduce-scatter.7.cloned.1.call-update) | async-done | bytes 32784 | tf_op jit(solution)/shard_map/reduce_scatter | solution.py:124
  293.6 42.9 %all-gather.22.cloned.1.call-done = f32[2048,128]{1,0:T(8,128)} async-done(((f32[64,128]{1,0:T(8,128)}), f32[2048,128]{1,0:T(8,128)}) %all-gather.22.cloned.1.call-update) | async-done | bytes 1048592 | tf_op jit(solution)/shard_map/all_gather | solution.py:135
  336.6 3.6 fusion.36
  341.8 41.2 %all-gather.24.cloned.1.call-done = f32[2048,128]{1,0:T(8,128)} async-done(((f32[64,128]{1,0:T(8,128)}), f32[2048,128]{1,0:T(8,128)}) %all-gather.24.cloned.1.call-update) | async-done | bytes 1048592 | tf_op jit(solution)/shard_map/all_gather | solution.py:135
  383.0 3.6 fusion.35
  388.2 41.2 %all-gather.26.cloned.1.call-done = f32[2048,128]{1,0:T(8,128)} async-done(((f32[64,128]{1,0:T(8,128)}), f32[2048,128]{1,0:T(8,128)}) %all-gather.26.cloned.1.call-update) | async-done | bytes 1048592 | tf_op jit(solution)/shard_map/all_gather | solution.py:135
  429.4 3.6 fusion.34
  434.6 41.2 %all-gather.28.cloned.1.call-done = f32[2048,128]{1,0:T(8,128)} async-done(((f32[64,128]{1,0:T(8,128)}), f32[2048,128]{1,0:T(8,128)}) %all-gather.28.cloned.1.call-update) | async-done | bytes 1048592 | tf_op jit(solution)/shard_map/all_gather | solution.py:135
  475.9 3.6 fusion.33
  481.3 41.0 %all-gather.30.cloned.1.call-done = f32[2048,128]{1,0:T(8,128)} async-done(((f32[64,128]{1,0:T(8,128)}), f32[2048,128]{1,0:T(8,128)}) %all-gather.30.cloned.1.call-update) | async-done | bytes 1048592 | tf_op jit(solution)/shard_map/all_gather | solution.py:135
  522.3 3.6 fusion.32
  526.3 2.4 fusion.31
  528.8 75.1 %reduce-scatter.9.cloned.1.call-done = f32[1,64,128]{2,1,0:T(8,128)} async-done(((f32[32,64,128]{2,1,0:T(8,128)}), f32[1,64,128]{2,1,0:T(8,128)}) %reduce-scatter.9.cloned.1.call-update) | async-done | bytes 32784 | tf_op jit(solution)/shard_map/reduce_scatter | solution.py:143
  604.9 2.4 fusion.30
  607.4 77.8 %reduce-scatter.11.cloned.1.call-done = f32[1,64,128]{2,1,0:T(8,128)} async-done(((f32[32,64,128]{2,1,0:T(8,128)}), f32[1,64,128]{2,1,0:T(8,128)}) %reduce-scatter.11.cloned.1.call-update) | async-done | bytes 32784 | tf_op jit(solution)/shard_map/reduce_scatter | solution.py:143
  686.1 2.4 fusion.29
  688.6 77.6 %reduce-scatter.13.cloned.1.call-done = f32[1,64,128]{2,1,0:T(8,128)} async-done(((f32[32,64,128]{2,1,0:T(8,128)}), f32[1,64,128]{2,1,0:T(8,128)}) %reduce-scatter.13.cloned.1.call-update) | async-done | bytes 32784 | tf_op jit(solution)/shard_map/reduce_scatter | solution.py:143
  767.2 2.4 fusion.28
  769.6 77.8 %reduce-scatter.15.cloned.1.call-done = f32[1,64,128]{2,1,0:T(8,128)} async-done(((f32[32,64,128]{2,1,0:T(8,128)}), f32[1,64,128]{2,1,0:T(8,128)}) %reduce-scatter.15.cloned.1.call-update) | async-done | bytes 32784 | tf_op jit(solution)/shard_map/reduce_scatter | solution.py:143
  848.4 2.4 fusion.27
  850.9 77.5 %reduce-scatter.17.cloned.1.call-done = f32[1,64,128]{2,1,0:T(8,128)} async-done(((f32[32,64,128]{2,1,0:T(8,128)}), f32[1,64,128]{2,1,0:T(8,128)}) %reduce-scatter.17.cloned.1.call-update) | async-done | bytes 32784 | tf_op jit(solution)/shard_map/reduce_scatter | solution.py:143
  928.4 1.6 convolution_select_fusion
  930.0 45.2 %all-gather.32.cloned.1.call-done = f32[2048,128]{1,0:T(8,128)} async-done(((f32[64,128]{1,0:T(8,128)}), f32[2048,128]{1,0:T(8,128)}) %all-gather.32.cloned.1.call-update) | async-done | bytes 1048592 | tf_op jit(solution)/shard_map/all_gather | solution.py:145
  975.2 1.5 concatenate.3
  976.6 93.5 %while.31 = (s32[]{:T(128)}, f32[64,64,128]{2,1,0:T(8,128)S(1)}, f32[32,64,128]{2,1,0:T(8,128)S(1)}, s32[32,3]{1,0:T(8,128)S(1)}, f32[32,3,128,128]{3,2,1,0:T(8,...) while((s32[]{:T(128)}, f32[64,64,128]{2,1,0:T(8,128)S(1)}, ...), condition=%wide.region_10.11_spmd, body=%wide.region_9.10_spmd.sunk | while | flops 50365472 | bytes 693510 | solution.py:78
  983.1 1.2 fusion.103
  989.0 1.2 fusion.103
  (363 shorter events, 162.8 us)
Async XLA Ops:
  7.2 2.3 copy-start.10
  7.2 36.5 %all-gather.18.cloned.1.call-start = ((), (), s32[]{:S(2)}) async-start(), calls=%async_computation.8 | async-start | bytes 2621440 | tf_op jit(solution)/shard_map/all_gather | solution.py:113
  7.9 103.2 %all-gather.16.cloned.1.call-start = ((), (), s32[]{:S(2)}) async-start(), calls=%async_computation.7 | async-start | bytes 7864320 | tf_op jit(solution)/shard_map/all_gather | solution.py:112
  8.7 214.9 %all-gather.20.cloned.1.call-start = ((), (), s32[]{:S(2)}) async-start(), calls=%async_computation.10 | async-start | bytes 2621440 | tf_op jit(solution)/shard_map/all_gather | solution.py:114
  9.4 280.6 %reduce-scatter.7.cloned.1.call-start = ((), (), s32[]{:S(2)}) async-start(), calls=%async_computation.9 | async-start | bytes 1081344 | tf_op jit(solution)/shard_map/reduce_scatter | solution.py:124
  212.0 2.5 copy-start.9
  223.5 66.4 %copy-start.8 = (f32[1,64,128]{2,1,0:T(8,128)S(1)}, f32[1,64,128]{2,1,0:T(8,128)}, u32[]{:S(2)}) copy-start(f32[1,64,128]{2,1,0:T(8,128)} %param.12) | copy-start | bytes 98308
  223.5 70.1 %all-to-all-start = ((f32[32,1,128,128]{3,2,1,0:T(8,128)}), f32[32,1,128,128]{3,2,1,0:T(8,128)S(1)}, u32[]{:S(2)}, u32[]{:S(2)}) async-start(f32[32,1,128,128]{3,2,1,0:T(8,128)} %all-gather.20.cloned.1.call-done), calls=%async_computation.1 | async-start | bytes 4194304 | tf_op jit(solution)/shard_map/all_to_all | solution.py:127
  234.2 102.3 %all-gather.22.cloned.1.call-start = ((), (), s32[]{:S(2)}) async-start(), calls=%async_computation.16 | async-start | bytes 1081344 | tf_op jit(solution)/shard_map/all_gather | solution.py:135
  291.6 48.6 %copy-start.4 = (f32[64,128]{1,0:T(8,128)S(1)}, f32[64,128]{1,0:T(8,128)}, u32[]{:S(2)}) copy-start(f32[64,128]{1,0:T(8,128)} %convolution_select_fusion.11) | copy-start | bytes 98308
  291.6 91.4 %all-gather.24.cloned.1.call-start = ((), (), s32[]{:S(2)}) async-start(), calls=%async_computation.17 | async-start | bytes 1081344 | tf_op jit(solution)/shard_map/all_gather | solution.py:135
  341.0 45.6 %copy-start.1 = (f32[64,128]{1,0:T(8,128)S(1)}, f32[64,128]{1,0:T(8,128)}, u32[]{:S(2)}) copy-start(f32[64,128]{1,0:T(8,128)} %convolution_select_fusion.10) | copy-start | bytes 98308
  341.0 88.4 %all-gather.26.cloned.1.call-start = ((), (), s32[]{:S(2)}) async-start(), calls=%async_computation.18 | async-start | bytes 1081344 | tf_op jit(solution)/shard_map/all_gather | solution.py:135
  387.4 45.6 %copy-start.2 = (f32[64,128]{1,0:T(8,128)S(1)}, f32[64,128]{1,0:T(8,128)}, u32[]{:S(2)}) copy-start(f32[64,128]{1,0:T(8,128)} %convolution_select_fusion.9) | copy-start | bytes 98308
  387.5 88.4 %all-gather.28.cloned.1.call-start = ((), (), s32[]{:S(2)}) async-start(), calls=%async_computation.19 | async-start | bytes 1081344 | tf_op jit(solution)/shard_map/all_gather | solution.py:135
  433.9 45.6 %copy-start.3 = (f32[64,128]{1,0:T(8,128)S(1)}, f32[64,128]{1,0:T(8,128)}, u32[]{:S(2)}) copy-start(f32[64,128]{1,0:T(8,128)} %convolution_select_fusion.8) | copy-start | bytes 98308
  433.9 88.4 %all-gather.30.cloned.1.call-start = ((), (), s32[]{:S(2)}) async-start(), calls=%async_computation.20 | async-start | bytes 1081344 | tf_op jit(solution)/shard_map/all_gather | solution.py:135
  480.3 45.6 %copy-start = (f32[64,128]{1,0:T(8,128)S(1)}, f32[64,128]{1,0:T(8,128)}, u32[]{:S(2)}) copy-start(f32[64,128]{1,0:T(8,128)} %convolution_select_fusion.7) | copy-start | bytes 98308
  480.3 123.6 %reduce-scatter.9.cloned.1.call-start = ((), (), s32[]{:S(2)}) async-start(), calls=%async_computation.11 | async-start | bytes 1081344 | tf_op jit(solution)/shard_map/reduce_scatter | solution.py:143
  528.8 156.4 %reduce-scatter.11.cloned.1.call-start = ((), (), s32[]{:S(2)}) async-start(), calls=%async_computation.12 | async-start | bytes 1081344 | tf_op jit(solution)/shard_map/reduce_scatter | solution.py:143
  604.9 80.3 %copy-start.5 = (f32[1,64,128]{2,1,0:T(8,128)S(1)}, f32[1,64,128]{2,1,0:T(8,128)}, u32[]{:S(2)}) copy-start(f32[1,64,128]{2,1,0:T(8,128)} %reduce-scatter.9.cloned.1.call-done) | copy-start | bytes 98308
  607.3 158.9 %reduce-scatter.13.cloned.1.call-start = ((), (), s32[]{:S(2)}) async-start(), calls=%async_computation.13 | async-start | bytes 1081344 | tf_op jit(solution)/shard_map/reduce_scatter | solution.py:143
  686.1 80.1 %copy-start.6 = (f32[1,64,128]{2,1,0:T(8,128)S(1)}, f32[1,64,128]{2,1,0:T(8,128)}, u32[]{:S(2)}) copy-start(f32[1,64,128]{2,1,0:T(8,128)} %reduce-scatter.11.cloned.1.call-done) | copy-start | bytes 98308
  688.5 158.9 %reduce-scatter.15.cloned.1.call-start = ((), (), s32[]{:S(2)}) async-start(), calls=%async_computation.14 | async-start | bytes 1081344 | tf_op jit(solution)/shard_map/reduce_scatter | solution.py:143
  769.6 158.8 %reduce-scatter.17.cloned.1.call-start = ((), (), s32[]{:S(2)}) async-start(), calls=%async_computation.15 | async-start | bytes 1081344 | tf_op jit(solution)/shard_map/reduce_scatter | solution.py:143
  848.4 80.0 %copy-start.7 = (f32[1,64,128]{2,1,0:T(8,128)S(1)}, f32[1,64,128]{2,1,0:T(8,128)}, u32[]{:S(2)}) copy-start(f32[1,64,128]{2,1,0:T(8,128)} %reduce-scatter.15.cloned.1.call-done) | copy-start | bytes 98308
  850.8 124.3 %all-gather.32.cloned.1.call-start = ((), (), s32[]{:S(2)}) async-start(), calls=%async_computation.21 | async-start | bytes 1081344 | tf_op jit(solution)/shard_map/all_gather | solution.py:145
Sparse Core Ops, SparseCore 0:
  9.6 34.0 all-gather.17
  45.4 65.7 all-gather.15
  112.8 31.4 all-gather.19
  213.3 76.6 reduce-scatter.6
  292.6 43.8 all-gather.21
  341.1 41.7 all-gather.23
  387.6 41.7 all-gather.25
  434.0 41.7 all-gather.27
  480.5 41.7 all-gather.29
  528.9 75.0 reduce-scatter.8
  608.0 77.0 reduce-scatter.10
  689.1 77.0 reduce-scatter.12
  770.3 77.1 reduce-scatter.14
  851.4 77.0 reduce-scatter.16
  931.1 44.0 all-gather.31
where the time goes:
time: 1080 us
  waiting for transfers between devices  798 us (74%)
  matrix products  189 us (18%)
  other arithmetic  25.3 us (2%)
  local copies, waits for them, and re-layouts  23 us (2%)
  between operations  18.4 us (2%)
  starting transfers between devices  11.5 us (1%)
    reduce_scatter x5, waiting for transfers between devices, local(): lax.psum_scatter(stacked, 'sn', scatter_dimension=0, tiled=True)  386 us
    all_gather x5, waiting for transfers between devices, local(): lax.all_gather(stacked, 'sn', axis=0, tiled=True)  208 us
    all_gather x1, waiting for transfers between devices, local(): lax.all_gather(leaf_blocks, 'rhs', axis=2, tiled=True)  67.4 us
    reduce_scatter x1, waiting for transfers between devices, local(): lax.psum_scatter(leaf_updates, 'sn', scatter_dimension=0, tiled=True)  55.7 us
    all_gather x1, waiting for transfers between devices, local(): all_top = lax.all_gather(backward_own[None], 'sn', axis=0, tiled=True)  45.2 us
    dot_general x32, matrix products, advance(): jnp.einsum('ck,rik->rci', solved, lax.dynamic_index_in_dim(blocks, positi...  41.9 us
    dot_general x32, matrix products, retreat(): jnp.einsum('rci,rik->ck', ancestors, lax.dynamic_index_in_dim(blocks, pos...  39.4 us
    dot_general x32, matrix products, advance(): jnp.einsum('ck,ik->ci', source, lax.dynamic_index_in_dim(inverses, positi...  35.3 us
  transfers between devices with their start and end apart: 16, of which 14 were waited for; matrix products, arithmetic and copies ran while one was open for 10% of the time, Pallas kernels for 0%

commit v1 on v0

--- a/solution.py
+++ b/solution.py
@@ -132,7 +132,9 @@
         own_inverse,
         my_level,
         levels,
-        lambda stacked: lax.all_gather(stacked, "sn", axis=0, tiled=True),
+        lambda stacked: jnp.concatenate(
+            lax.all_to_all(jnp.stack([stacked] * lax.axis_size("sn")), "sn", 0, 0), axis=0
+        ),
     )
     backward_own = backward_by_rows(
         forward_own,

time: 1080 us -> 1140 us (1.056)
  waiting for transfers between devices: 798 us -> 702 us
  local copies, waits for them, and re-layouts: 23 us -> 84.8 us
  other arithmetic: 25.3 us -> 69 us
  matrix products: 189 us -> 220 us
  starting transfers between devices: 11.5 us -> 31.5 us
    all_gather x5 -> x0, waiting for transfers between devices: 208 us -> none  [local(): lax.all_gather(stacked, 'sn', axis=0, tiled=True)]
    all_to_all x0 -> x5, waiting for transfers between devices: none -> 79.8 us  [local(): lax.all_to_all(jnp.stack([stacked] * lax.axis_size('sn')), 'sn', 0, 0)]
    gather x32, local copies, waits for them, and re-layouts: 17.8 us -> 68.5 us  [retreat(): ancestors = jnp.take(solution_buffer, targets, axis=0)]
    scatter-add x32, other arithmetic: 21.6 us -> 65.5 us  [advance(): updates = updates.at[targets].add(outgoing)]
    all_gather x1, waiting for transfers between devices: 0.01 us -> 34.2 us  [local(): lax.all_gather(top_blocks, 'rhs', axis=2, tiled=True)]
    all_to_all x0 -> x5, starting transfers between devices: none -> 23.2 us  [local(): lax.all_to_all(jnp.stack([stacked] * lax.axis_size('sn')), 'sn', 0, 0)]
    dot_general x32, matrix products: 35.3 us -> 55.5 us  [advance(): jnp.einsum('ck,ik->ci', source, lax.dynamic_index_in_dim(inverses, positi...]
    dot_general x32, matrix products: 32.9 us -> 52.6 us  [retreat(): jnp.einsum('ci,ik->ck', own_rhs - summed, lax.dynamic_index_in_dim(invers...]
  transfers between devices with their start and end apart: 16 -> 16, of which waited for: 14 -> 15; matrix products, arithmetic and copies ran while one was open for 10% -> 15% of each run, Pallas kernels for 0% -> 0%
where the time goes in v1:
time: 1140 us
  waiting for transfers between devices  702 us (62%)
  matrix products  220 us (19%)
  local copies, waits for them, and re-layouts  84.8 us (7%)
  other arithmetic  69 us (6%)
  starting transfers between devices  31.5 us (3%)
  between operations  18.4 us (2%)
    reduce_scatter x5, waiting for transfers between devices, local(): lax.psum_scatter(stacked, 'sn', scatter_dimension=0, tiled=True)  382 us
    all_to_all x5, waiting for transfers between devices, local(): lax.all_to_all(jnp.stack([stacked] * lax.axis_size('sn')), 'sn', 0, 0)  79.8 us
    gather x32, local copies, waits for them, and re-layouts, retreat(): ancestors = jnp.take(solution_buffer, targets, axis=0)  68.5 us
    all_gather x1, waiting for transfers between devices, local(): lax.all_gather(leaf_blocks, 'rhs', axis=2, tiled=True)  67.4 us
    reduce_scatter x1, waiting for transfers between devices, local(): lax.psum_scatter(leaf_updates, 'sn', scatter_dimension=0, tiled=True)  66.4 us
    scatter-add x32, other arithmetic, advance(): updates = updates.at[targets].add(outgoing)  65.5 us
    dot_general x32, matrix products, advance(): jnp.einsum('ck,ik->ci', source, lax.dynamic_index_in_dim(inverses, positi...  55.5 us
    dot_general x32, matrix products, retreat(): jnp.einsum('ci,ik->ck', own_rhs - summed, lax.dynamic_index_in_dim(invers...  52.6 us
  transfers between devices with their start and end apart: 16, of which 15 were waited for; matrix products, arithmetic and copies ran while one was open for 15% of the time, Pallas kernels for 0%

profile of v1, /device:TPU:1, one launch (start us, length us, event | category | flops | bytes accessed | tf_op | source)
XLA Modules:
  0.0 1135.5 jit_solution(7036593655733570670)
XLA Ops:
  9.5 34.2 %all-gather.10.cloned.1.call-done = f32[32,1,128,128]{3,2,1,0:T(8,128)} async-done(((f32[32,1,32,128]{3,2,1,0:T(8,128)}), f32[32,1,128,128]{3,2,1,0:T(8,128)}) %all-gather.10.cloned.1.call-update) | async-done | bytes 2097168 | tf_op jit(solution)/shard_map/all_gather | solution.py:114
  43.7 7.7 all-to-all-start.1
  51.5 24.8 %all-gather.8.cloned.1.call-done = f32[32,128,128]{2,1,0:T(8,128)} async-done(((f32[32,32,128]{2,1,0:T(8,128)}), f32[32,128,128]{2,1,0:T(8,128)}) %all-gather.8.cloned.1.call-update) | async-done | bytes 2097168 | tf_op jit(solution)/shard_map/all_gather | solution.py:113
  76.3 67.4 %all-gather.6.cloned.1.call-done = f32[32,3,128,128]{3,2,1,0:T(8,128)} async-done(((f32[32,3,32,128]{3,2,1,0:T(8,128)}), f32[32,3,128,128]{3,2,1,0:T(8,128)}) %all-gather.6.cloned.1.call-update) | async-done | bytes 6291472 | tf_op jit(solution)/shard_map/all_gather | solution.py:112
  145.3 163.1 %while.30 = (s32[]{:T(128)}, f32[64,64,128]{2,1,0:T(8,128)}, f32[32,64,128]{2,1,0:T(8,128)}, s32[32,3]{1,0:T(8,128)S(1)}, f32[32,3,128,128]{3,2,1,0:T(8,128)}, /...) while((s32[]{:T(128)}, f32[64,64,128]{2,1,0:T(8,128)}, f32[32,64,128]{2,1,0:T(8,128)}, ...), condition=%wide.region_2.3_spmd, body=%wide.region_0.2_spmd.sunk | while | flops 50364424 | bytes 820873 | solution.py:51
  308.4 2.4 slice.6
  312.1 9.0 all_gather.17
  321.1 66.4 %reduce-scatter.7.cloned.1.call-done = f32[1,64,128]{2,1,0:T(8,128)} async-done(((f32[32,64,128]{2,1,0:T(8,128)}), f32[1,64,128]{2,1,0:T(8,128)}) %reduce-scatter.7.cloned.1.call-update) | async-done | bytes 32784 | tf_op jit(solution)/shard_map/reduce_scatter | solution.py:124
  389.7 7.5 all-to-all-start
  399.1 15.0 %all-to-all-done = f32[32,1,64,128]{3,2,1,0:T(8,128)S(1)} async-done(((f32[32,1,64,128]{3,2,1,0:T(8,128)}), f32[32,1,64,128]{3,2,1,0:T(8,128)S(1)}, u32[]{:S(2)}, u32[]{:S(2)}) %all-to-all-start) | async-done | bytes 1048608 | tf_op jit(solution)/shard_map/all_to_all | solution.py:136
  414.1 2.3 fusion.84
  417.9 3.9 all-to-all-start.2
  422.4 16.3 %all-to-all-done.2 = f32[32,1,64,128]{3,2,1,0:T(8,128)S(1)} async-done(((f32[32,1,64,128]{3,2,1,0:T(8,128)}), f32[32,1,64,128]{3,2,1,0:T(8,128)S(1)}, u32[]{:S(2)}, u32[]{:S(2)}) %all-to-all-start.2) | async-done | bytes 1048608 | tf_op jit(solution)/shard_map/all_to_all | solution.py:136
  438.7 2.3 fusion.81
  442.5 3.9 all-to-all-start.3
  447.0 16.3 %all-to-all-done.3 = f32[32,1,64,128]{3,2,1,0:T(8,128)S(1)} async-done(((f32[32,1,64,128]{3,2,1,0:T(8,128)}), f32[32,1,64,128]{3,2,1,0:T(8,128)S(1)}, u32[]{:S(2)}, u32[]{:S(2)}) %all-to-all-start.3) | async-done | bytes 1048608 | tf_op jit(solution)/shard_map/all_to_all | solution.py:136
  463.3 2.3 fusion.78
  467.1 3.9 all-to-all-start.4
  471.7 16.3 %all-to-all-done.4 = f32[32,1,64,128]{3,2,1,0:T(8,128)S(1)} async-done(((f32[32,1,64,128]{3,2,1,0:T(8,128)}), f32[32,1,64,128]{3,2,1,0:T(8,128)S(1)}, u32[]{:S(2)}, u32[]{:S(2)}) %all-to-all-start.4) | async-done | bytes 1048608 | tf_op jit(solution)/shard_map/all_to_all | solution.py:136
  487.9 2.3 fusion.75
  491.7 3.9 all-to-all-start.5
  496.5 16.0 %all-to-all-done.5 = f32[32,1,64,128]{3,2,1,0:T(8,128)S(1)} async-done(((f32[32,1,64,128]{3,2,1,0:T(8,128)}), f32[32,1,64,128]{3,2,1,0:T(8,128)S(1)}, u32[]{:S(2)}, u32[]{:S(2)}) %all-to-all-start.5) | async-done | bytes 1048608 | tf_op jit(solution)/shard_map/all_to_all | solution.py:136
  512.5 2.3 fusion.72
  515.3 2.5 fusion.48
  517.9 73.7 %reduce-scatter.9.cloned.1.call-done = f32[1,64,128]{2,1,0:T(8,128)} async-done(((f32[32,64,128]{2,1,0:T(8,128)}), f32[1,64,128]{2,1,0:T(8,128)}) %reduce-scatter.9.cloned.1.call-update) | async-done | bytes 32784 | tf_op jit(solution)/shard_map/reduce_scatter | solution.py:145
  592.5 2.5 fusion.50
  595.1 77.1 %reduce-scatter.11.cloned.1.call-done = f32[1,64,128]{2,1,0:T(8,128)} async-done(((f32[32,64,128]{2,1,0:T(8,128)}), f32[1,64,128]{2,1,0:T(8,128)}) %reduce-scatter.11.cloned.1.call-update) | async-done | bytes 32784 | tf_op jit(solution)/shard_map/reduce_scatter | solution.py:145
  673.2 2.5 fusion.52
  675.7 77.2 %reduce-scatter.13.cloned.1.call-done = f32[1,64,128]{2,1,0:T(8,128)} async-done(((f32[32,64,128]{2,1,0:T(8,128)}), f32[1,64,128]{2,1,0:T(8,128)}) %reduce-scatter.13.cloned.1.call-update) | async-done | bytes 32784 | tf_op jit(solution)/shard_map/reduce_scatter | solution.py:145
  753.9 2.5 fusion.54
  756.5 77.2 %reduce-scatter.15.cloned.1.call-done = f32[1,64,128]{2,1,0:T(8,128)} async-done(((f32[32,64,128]{2,1,0:T(8,128)}), f32[1,64,128]{2,1,0:T(8,128)}) %reduce-scatter.15.cloned.1.call-update) | async-done | bytes 32784 | tf_op jit(solution)/shard_map/reduce_scatter | solution.py:145
  834.6 2.5 fusion.56
  837.2 77.2 %reduce-scatter.17.cloned.1.call-done = f32[1,64,128]{2,1,0:T(8,128)} async-done(((f32[32,64,128]{2,1,0:T(8,128)}), f32[1,64,128]{2,1,0:T(8,128)}) %reduce-scatter.17.cloned.1.call-update) | async-done | bytes 32784 | tf_op jit(solution)/shard_map/reduce_scatter | solution.py:145
  916.0 45.2 %all-gather.12.cloned.1.call-done = f32[2048,128]{1,0:T(8,128)} async-done(((f32[64,128]{1,0:T(8,128)}), f32[2048,128]{1,0:T(8,128)}) %all-gather.12.cloned.1.call-update) | async-done | bytes 1048592 | tf_op jit(solution)/shard_map/all_gather | solution.py:147
  961.1 2.9 concatenate.3
  964.0 162.4 %while.31 = (s32[]{:T(128)}, f32[64,64,128]{2,1,0:T(8,128)}, f32[32,64,128]{2,1,0:T(8,128)}, s32[32,3]{1,0:T(8,128)S(1)}, f32[32,3,128,128]{3,2,1,0:T(8,128)}, /...) while((s32[]{:T(128)}, f32[64,64,128]{2,1,0:T(8,128)}, ...), condition=%wide.region_10.11_spmd, body=%wide.region_9.10_spmd.sunk | while | flops 50365472 | bytes 693518 | solution.py:78
  964.0 2.1 gather_fusion
  969.1 2.1 gather_fusion
  974.1 2.1 gather_fusion
  979.2 2.1 gather_fusion
  984.3 2.1 gather_fusion
  989.4 2.1 gather_fusion
  994.4 2.1 gather_fusion
  999.5 2.1 gather_fusion
  1004.6 2.1 gather_fusion
  1009.7 2.1 gather_fusion
  1014.7 2.1 gather_fusion
  1019.8 2.1 gather_fusion
  1024.9 2.1 gather_fusion
  1030.0 2.1 gather_fusion
  1035.0 2.1 gather_fusion
  1040.1 2.1 gather_fusion
  1045.2 2.1 gather_fusion
  1050.3 2.1 gather_fusion
  1055.3 2.1 gather_fusion
  1060.4 2.1 gather_fusion
  1065.5 2.1 gather_fusion
  1070.6 2.1 gather_fusion
  1075.6 2.1 gather_fusion
  1080.7 2.1 gather_fusion
  1095.9 2.1 gather_fusion
  1101.0 2.1 gather_fusion
  1106.1 2.1 gather_fusion
  1126.4 2.3 slice.7
  (353 shorter events, 286.7 us)
Async XLA Ops:
  7.2 2.2 copy-start.5
  7.2 36.5 %all-gather.10.cloned.1.call-start = ((), (), s32[]{:S(2)}) async-start(), calls=%async_computation.15 | async-start | bytes 2621440 | tf_op jit(solution)/shard_map/all_gather | solution.py:114
  7.9 68.4 %all-gather.8.cloned.1.call-start = ((), (), s32[]{:S(2)}) async-start(), calls=%async_computation.13 | async-start | bytes 2621440 | tf_op jit(solution)/shard_map/all_gather | solution.py:113
  8.7 135.0 %all-gather.6.cloned.1.call-start = ((), (), s32[]{:S(2)}) async-start(), calls=%async_computation.12 | async-start | bytes 7864320 | tf_op jit(solution)/shard_map/all_gather | solution.py:112
  43.7 344.8 %all-to-all-start.1 = ((f32[32,1,128,128]{3,2,1,0:T(8,128)}), f32[32,1,128,128]{3,2,1,0:T(8,128)S(1)}, u32[]{:S(2)}, u32[]{:S(2)}) async-start(f32[32,1,128,128]{3,2,1,0:T(8,128)} %all-gather.10.cloned.1.call-done), calls=%async_computation.2 | async-start | bytes 4194304 | tf_op jit(solution)/shard_map/all_to_all | solution.py:127
  51.4 336.1 %reduce-scatter.7.cloned.1.call-start = ((), (), s32[]{:S(2)}) async-start(), calls=%async_computation.14 | async-start | bytes 1081344 | tf_op jit(solution)/shard_map/reduce_scatter | solution.py:124
  308.4 3.7 copy-start.4
  308.4 79.0 %copy-start.3 = (f32[1,64,128]{2,1,0:T(8,128)S(1)}, f32[1,64,128]{2,1,0:T(8,128)}, u32[]{:S(2)}) copy-start(f32[1,64,128]{2,1,0:T(8,128)} %param.12) | copy-start | bytes 98308
  389.7 24.4 %all-to-all-start = ((f32[32,1,64,128]{3,2,1,0:T(8,128)}), f32[32,1,64,128]{3,2,1,0:T(8,128)S(1)}, u32[]{:S(2)}, u32[]{:S(2)}) async-start(f32[32,1,64,128]{3,2,1,0:T(8,128)} %stack.15), calls=%async_computation.1 | async-start | bytes 2097152 | tf_op jit(solution)/shard_map/all_to_all | solution.py:136
  417.9 20.8 %all-to-all-start.2 = ((f32[32,1,64,128]{3,2,1,0:T(8,128)}), f32[32,1,64,128]{3,2,1,0:T(8,128)S(1)}, u32[]{:S(2)}, u32[]{:S(2)}) async-start(f32[32,1,64,128]{3,2,1,0:T(8,128)} %stack.16), calls=%async_computation.3 | async-start | bytes 2097152 | tf_op jit(solution)/shard_map/all_to_all | solution.py:136
  442.5 20.8 %all-to-all-start.3 = ((f32[32,1,64,128]{3,2,1,0:T(8,128)}), f32[32,1,64,128]{3,2,1,0:T(8,128)S(1)}, u32[]{:S(2)}, u32[]{:S(2)}) async-start(f32[32,1,64,128]{3,2,1,0:T(8,128)} %stack.17), calls=%async_computation.4 | async-start | bytes 2097152 | tf_op jit(solution)/shard_map/all_to_all | solution.py:136
  467.1 20.8 %all-to-all-start.4 = ((f32[32,1,64,128]{3,2,1,0:T(8,128)}), f32[32,1,64,128]{3,2,1,0:T(8,128)S(1)}, u32[]{:S(2)}, u32[]{:S(2)}) async-start(f32[32,1,64,128]{3,2,1,0:T(8,128)} %stack.18), calls=%async_computation.5 | async-start | bytes 2097152 | tf_op jit(solution)/shard_map/all_to_all | solution.py:136
  491.7 20.8 %all-to-all-start.5 = ((f32[32,1,64,128]{3,2,1,0:T(8,128)}), f32[32,1,64,128]{3,2,1,0:T(8,128)S(1)}, u32[]{:S(2)}, u32[]{:S(2)}) async-start(f32[32,1,64,128]{3,2,1,0:T(8,128)} %stack.19), calls=%async_computation.6 | async-start | bytes 2097152 | tf_op jit(solution)/shard_map/all_to_all | solution.py:136
  495.6 95.9 %reduce-scatter.9.cloned.1.call-start = ((), (), s32[]{:S(2)}) async-start(), calls=%async_computation.16 | async-start | bytes 1081344 | tf_op jit(solution)/shard_map/reduce_scatter | solution.py:145
  517.8 154.4 %reduce-scatter.11.cloned.1.call-start = ((), (), s32[]{:S(2)}) async-start(), calls=%async_computation.17 | async-start | bytes 1081344 | tf_op jit(solution)/shard_map/reduce_scatter | solution.py:145
  592.5 79.7 %copy-start = (f32[1,64,128]{2,1,0:T(8,128)S(1)}, f32[1,64,128]{2,1,0:T(8,128)}, u32[]{:S(2)}) copy-start(f32[1,64,128]{2,1,0:T(8,128)} %reduce-scatter.9.cloned.1.call-done) | copy-start | bytes 98308
  595.0 157.9 %reduce-scatter.13.cloned.1.call-start = ((), (), s32[]{:S(2)}) async-start(), calls=%async_computation.18 | async-start | bytes 1081344 | tf_op jit(solution)/shard_map/reduce_scatter | solution.py:145
  673.2 79.8 %copy-start.1 = (f32[1,64,128]{2,1,0:T(8,128)S(1)}, f32[1,64,128]{2,1,0:T(8,128)}, u32[]{:S(2)}) copy-start(f32[1,64,128]{2,1,0:T(8,128)} %reduce-scatter.11.cloned.1.call-done) | copy-start | bytes 98308
  675.7 158.0 %reduce-scatter.15.cloned.1.call-start = ((), (), s32[]{:S(2)}) async-start(), calls=%async_computation.19 | async-start | bytes 1081344 | tf_op jit(solution)/shard_map/reduce_scatter | solution.py:145
  756.4 158.0 %reduce-scatter.17.cloned.1.call-start = ((), (), s32[]{:S(2)}) async-start(), calls=%async_computation.20 | async-start | bytes 1081344 | tf_op jit(solution)/shard_map/reduce_scatter | solution.py:145
  834.6 79.8 %copy-start.2 = (f32[1,64,128]{2,1,0:T(8,128)S(1)}, f32[1,64,128]{2,1,0:T(8,128)}, u32[]{:S(2)}) copy-start(f32[1,64,128]{2,1,0:T(8,128)} %reduce-scatter.15.cloned.1.call-done) | copy-start | bytes 98308
  837.1 124.0 %all-gather.12.cloned.1.call-start = ((), (), s32[]{:S(2)}) async-start(), calls=%async_computation.21 | async-start | bytes 1081344 | tf_op jit(solution)/shard_map/all_gather | solution.py:147
Sparse Core Ops, SparseCore 0:
  9.6 34.0 all-gather.9
  45.4 30.8 all-gather.7
  77.9 65.7 all-gather.5
  311.0 76.4 reduce-scatter.6
  517.9 73.5 reduce-scatter.8
  595.1 77.0 reduce-scatter.10
  675.8 77.0 reduce-scatter.12
  756.5 77.0 reduce-scatter.14
  837.2 77.0 reduce-scatter.16
  917.0 44.0 all-gather.11
